TPU v7x, 256 devices: a whole 4x4x8 slice. The times are simulated.
256 devices in a mesh: seq: 64 (over z, x, core), tp: 4 (over y).
Axes of the slice: x: 4, y: 4, z: 8, core: 2. Of those that a mesh axis runs over, the one named last changes fastest.
Arguments:
- hidden: bfloat16 [32768, 4096], P(('seq', 'tp')), may hold values from -640 to 640
- norm_gain: float32 [4096], replicated, may hold values from 0.5 to 1.5
- w_query: bfloat16 [4096, 2048], P(None, 'tp'), may hold values from -0.078125 to 0.078125
- w_key: bfloat16 [4096, 1024], P(None, 'tp'), may hold values from -2.421875 to 2.421875
- w_value: bfloat16 [4096, 1024], P(None, 'tp'), may hold values from -0.09375 to 0.09375
- doc_start: int32 [32768], P('seq'), may hold values from 0 to 32767, as said below
- block_owner: int32 [1024], P('seq'), may hold values from 0 to 63, as said below
Outputs:
- context_rows: bfloat16 [32768, 2048], P(('seq', 'tp'))
- key_cache: bfloat16 [49152, 1024], P('seq', 'tp')
- value_cache: bfloat16 [49152, 1024], P('seq', 'tp')
Inputs may be any that keep to these rules, and one draw needn't show every extreme that they name: `doc_start`: rows with equal values form one document: consecutive rows beginning at the row whose number is that value. Every document has at most 256 rows and one has exactly 256; all but the last have at least 64. `block_owner`: owner numbers never fall along the blocks. Owner o holds the blocks from o * 16 + e(o) up to (o + 1) * 16 + e(o + 1) - 1, where -4 <= e <= 4 and e is 0 at both ends of the axis; so an owner holds between 8 and 24 blocks, and some owner holds exactly 24.
All inputs are finite; a program needn't handle non-finite values.
Results may differ from a plain program's by a relative error of at most 0.0078.
Values may be sent and summed in bfloat16 or wider, within the bound.
No kernel may reach another device: no remote copies, remote signals or barrier semaphores. Data moves between devices by JAX's collectives and lax.ppermute only.
A program may use at most 128 MiB of HBM per device.

v0:
```python
import jax
import jax.numpy as jnp
from jax import lax
from jax.sharding import PartitionSpec as P

HD = 128
DOC_MAX = 256
EPS = 1e-05
ROPE_BASE = 500000.0


def from_behind(array, axis, by):
    length = lax.axis_size(axis)
    pairs = [(i, i + by) for i in range(length) if 0 <= i + by < length]
    return lax.ppermute(array, axis, pairs)


def rotate(packed, positions, head_count):
    row_count = packed.shape[0]
    head_width = packed.shape[1] // head_count
    half_width = head_width // 2
    frequency = jnp.power(
        ROPE_BASE, -jnp.arange(half_width, dtype=jnp.float32) * (2.0 / head_width)
    )
    angles = positions.astype(jnp.float32)[:, None] * frequency[None, :]
    cosine = jnp.cos(angles)[:, None, :]
    sine_part = jnp.sin(angles)[:, None, :]
    reshaped = packed.reshape(row_count, head_count, head_width)
    first_half = reshaped[:, :, :half_width]
    second = reshaped[:, :, half_width:]
    rotated = jnp.concatenate(
        [first_half * cosine - second * sine_part, second * cosine + first_half * sine_part], axis=2
    )
    return rotated.reshape(row_count, head_count * head_width)


def project(rows_in, norm_gain, w_query, w_key, w_value, positions):
    widened = rows_in.astype(jnp.float32)
    inverse_rms = lax.rsqrt(jnp.mean(widened * widened, axis=1, keepdims=True) + EPS)
    normed = (widened * inverse_rms * norm_gain[None, :]).astype(jnp.bfloat16)
    queries = jnp.dot(normed, w_query, preferred_element_type=jnp.float32)
    keys_f = jnp.dot(normed, w_key, preferred_element_type=jnp.float32)
    values_f = jnp.dot(normed, w_value, preferred_element_type=jnp.float32)
    queries = rotate(queries, positions, queries.shape[1] // HD).astype(jnp.bfloat16)
    keys_f = rotate(keys_f, positions, keys_f.shape[1] // HD).astype(jnp.bfloat16)
    return (queries, keys_f, values_f.astype(jnp.bfloat16))


def attend(
    queries, keys_in, values_in, query_doc, query_row, key_doc, key_row, key_live, offset, reach
):
    row_count = queries.shape[0]
    groups = keys_in.shape[1] // HD
    per_group = queries.shape[1] // keys_in.shape[1]
    window = row_count + reach

    def one_tile(index):
        first = index * row_count
        key_first = first + offset - reach
        near_keys = lax.dynamic_slice_in_dim(keys_in, key_first, window, 0)
        near_values = lax.dynamic_slice_in_dim(values_in, key_first, window, 0)
        near_doc = lax.dynamic_slice_in_dim(key_doc, key_first, window, 0)
        near_row = lax.dynamic_slice_in_dim(key_row, key_first, window, 0)
        near_live = lax.dynamic_slice_in_dim(key_live, key_first, window, 0)
        query_four = queries.reshape(row_count, groups, per_group, HD)
        key_three = near_keys.reshape(window, groups, HD)
        value_three = near_values.reshape(window, groups, HD)
        scores = jnp.einsum(
            "rgjd,kgd->gjrk", query_four, key_three, preferred_element_type=jnp.float32
        ) * HD ** (-0.5)
        allowed = (
            (query_doc[:, None] == near_doc[None, :])
            & (near_row[None, :] <= query_row[:, None])
            & (near_live[None, :] > 0)
        )
        allowed = allowed | (jnp.arange(window)[None, :] == jnp.arange(row_count)[:, None] + reach)
        scores = jnp.where(allowed[None, None], scores, -jnp.inf)
        highest = jnp.max(scores, axis=3, keepdims=True)
        weights = jnp.exp(scores - highest)
        weights = (weights / jnp.sum(weights, axis=3, keepdims=True)).astype(jnp.bfloat16)
        blended = jnp.einsum(
            "gjrk,kgd->rgjd", weights, value_three, preferred_element_type=jnp.float32
        )
        return blended.astype(jnp.bfloat16).reshape(row_count, groups * per_group * HD)

    tiles = lax.map(one_tile, jnp.arange(row_count // row_count, dtype=jnp.int32))
    return tiles.reshape(row_count, queries.shape[1])


def shards(hidden, norm_gain, w_query, w_key, w_value, doc_start, block_owner):
    home_hidden = lax.all_gather(hidden, "tp", axis=0, tiled=True)
    my_index = lax.axis_index("seq")
    home_rows = home_hidden.shape[0]
    home_blocks = block_owner.shape[0]
    block_rows = home_rows // home_blocks
    spill_rows = home_blocks // 4 * block_rows
    frame_size = home_rows + 2 * spill_rows
    all_rows = lax.axis_size("seq") * home_rows
    row_number = my_index * home_rows + jnp.arange(home_rows, dtype=jnp.int32)
    row_owner = jnp.repeat(block_owner, block_rows)
    frame_number = my_index * home_rows - spill_rows + jnp.arange(frame_size, dtype=jnp.int32)
    queries, keys_own, values_own = project(
        home_hidden, norm_gain, w_query, w_key, w_value, row_number - doc_start
    )
    left = from_behind((keys_own, values_own, doc_start), "seq", 1)
    left_live = jnp.ones((home_rows,), jnp.int32) * (my_index > 0).astype(jnp.int32)
    home_context = attend(
        queries,
        jnp.concatenate([left[0], keys_own], axis=0),
        jnp.concatenate([left[1], values_own], axis=0),
        doc_start,
        row_number,
        jnp.concatenate([left[2], doc_start], axis=0),
        jnp.concatenate([row_number - home_rows, row_number], axis=0),
        jnp.concatenate([left_live, jnp.ones((home_rows,), jnp.int32)], axis=0),
        home_rows,
        DOC_MAX,
    )
    arrived = []
    for direction in (1, -1):
        low_row = home_rows - spill_rows if direction == 1 else 0
        payload = (
            keys_own[low_row : low_row + spill_rows],
            values_own[low_row : low_row + spill_rows],
            row_owner[low_row : low_row + spill_rows],
        )
        arrived.append(from_behind((payload[0], payload[1], payload[2]), "seq", direction))
    from_left, from_right = arrived
    frame_keys = jnp.concatenate([from_left[0], keys_own, from_right[0]], axis=0)
    frame_values = jnp.concatenate([from_left[1], values_own, from_right[1]], axis=0)
    frame_owner = jnp.concatenate([from_left[2], row_owner, from_right[2]], axis=0)
    frame_live = (
        (frame_owner == my_index) & (frame_number >= 0) & (frame_number < all_rows)
    ).astype(jnp.int32)
    live_column = frame_live[:, None] > 0
    key_cache = jnp.where(live_column, frame_keys, jnp.zeros((), jnp.bfloat16))
    value_cache = jnp.where(live_column, frame_values, jnp.zeros((), jnp.bfloat16))
    context_rows = lax.all_to_all(home_context, "tp", split_axis=0, concat_axis=1, tiled=True)
    return (context_rows, key_cache, value_cache)


def solution(mesh):
    return jax.shard_map(
        shards,
        mesh=mesh,
        in_specs=(
            P(("seq", "tp"), None),
            P(),
            P(None, "tp"),
            P(None, "tp"),
            P(None, "tp"),
            P("seq"),
            P("seq"),
        ),
        out_specs=(P(("seq", "tp"), None), P("seq", "tp"), P("seq", "tp")),
        check_vma=False,
    )
```

profile of v0, /device:TPU:128, one launch (start us, length us, event | category | flops | bytes accessed | tf_op | source)
XLA Modules:
  0.0 141.9 jit_solution(14735143676403520581)
XLA Ops:
  7.9 0.8 fusion.35
  8.9 3.6 %collective-permute-start.4 = (s32[128]{0:T(128)S(1)}, s32[128]{0:T(128)S(1)}, u32[]{:S(2)}, u32[]{:S(2)}) collective-permute-start(s32[128]{0:T(128)S(1)} %slice.56), channel_id=1, source_target_pairs={{4,0},{8,4},{12,8},{16,12},{20,16},{24,20},{28,24},{32,28},{36,32}... | collective-permute-start | bytes 1544 | tf_op jit(solution)/shard_map/ppermute | solution.py:15
  12.7 1.9 %collective-permute-start.3 = (s32[128]{0:T(128)S(1)}, s32[128]{0:T(128)S(1)}, u32[]{:S(2)}, u32[]{:S(2)}) collective-permute-start(s32[128]{0:T(128)S(1)} %slice.54), channel_id=1, source_target_pairs={{0,4},{4,8},{8,12},{12,16},{16,20},{20,24},{24,28},{28,32},{32,36}... | collective-permute-start | bytes 1544 | tf_op jit(solution)/shard_map/ppermute | solution.py:15
  14.6 1.9 %collective-permute-start.1 = (s32[512]{0:T(512)}, s32[512]{0:T(512)S(1)}, u32[]{:S(2)}, u32[]{:S(2)}) collective-permute-start(s32[512]{0:T(512)} %param.12), channel_id=1, source_target_pairs={{0,4},{4,8},{8,12},{12,16},{16,20},{20,24},{24,28},{28,32},{32,36}... | collective-permute-start | bytes 6152 | tf_op jit(solution)/shard_map/ppermute | solution.py:15
  17.9 0.7 broadcast_in_dim.78
  18.7 0.8 copy.30
  19.5 0.8 copy.32
  20.9 2.1 %collective-permute-done.1 = s32[512]{0:T(512)S(1)} collective-permute-done((s32[512]{0:T(512)}, s32[512]{0:T(512)S(1)}, u32[]{:S(2)}, u32[]{:S(2)}) %collective-permute-start.1) | collective-permute-done | bytes 2080 | tf_op jit(solution)/shard_map/ppermute | solution.py:15
  23.8 2.2 %fusion.9 = pred[512,768]{0,1:T(8,128)(4,1)} fusion(s32[512]{0:T(512)S(1)} %iota_add_fusion.1, s32[512]{0:T(512)S(1)} %get-tuple-element.62, s32[512]{0:T(512)} %param.12, s32[768]{0:T(1024)S(1)} %dynamic_slice.25, s32[768]{0:T(1024)S(1)} %dynamic_slice.24, pred[768]{0:T(1024)(128)(4,1)S(1)} %slice_compare_fusion), kind=kLoop, calls=%fused_computation.15 | loop fusion | flops 2359296 | bytes 406272 | tf_op jit(solution)/shard_map/while/body/eval_jaxpr/or | solution.py:76
  25.9 36.2 %all-gather.2.cloned.1.call-done = bf16[512,4096]{1,0:T(8,128)(2,1)} async-done(((bf16[128,4096]{1,0:T(8,128)(2,1)}), bf16[512,4096]{1,0:T(8,128)(2,1)}) %all-gather.2.cloned.1.call-update) | async-done | bytes 4194320 | tf_op jit(solution)/shard_map/all_gather | solution.py:91
  62.1 3.2 %fusion.1 = f32[512]{0:T(512)S(1)} fusion(bf16[512,4096]{1,0:T(8,128)(2,1)} %all-gather.2.cloned.1.call-done), kind=kLoop, calls=%fused_computation.3 | loop fusion | flops 6290944 | bytes 4196352 | tf_op jit(solution)/shard_map/reduce_sum | solution.py:39
  65.6 2.0 %convolution_convert_fusion = bf16[512,256]{1,0:T(8,128)(2,1)} fusion(bf16[4096,256]{1,0:T(8,128)(2,1)S(1)} %copy-done, bf16[512,4096]{1,0:T(8,128)(2,1)S(1)} %copy-done.1, f32[4096]{0:T(1024)S(1)} %copy-done.4, f32[512]{0:T(512)S(1)} %add_rsqrt_fusion), kind=kOutput, calls=%fused_computation.18 | convolution fusion | flops 1082261504 | bytes 6572032 | tf_op jit(solution)/shard_map/dot_general | solution.py:43
  67.6 0.9 fusion.34
  68.5 1.9 %collective-permute-start = (bf16[512,256]{1,0:T(8,128)(2,1)}, bf16[512,256]{1,0:T(8,128)(2,1)}, u32[]{:S(2)}, u32[]{:S(2)}) collective-permute-start(bf16[512,256]{1,0:T(8,128)(2,1)} %convolution_convert_fusion), channel_id=1, source_target_pairs={{0,4},{4,8},{8,12},{12,16},{16,20},{20,24},{24,28},{28,32},{32,36}... | collective-permute-start | bytes 786440 | tf_op jit(solution)/shard_map/ppermute | solution.py:15
  70.5 3.5 %collective-permute-start.7 = (bf16[128,256]{1,0:T(8,128)(2,1)S(1)}, bf16[128,256]{1,0:T(8,128)(2,1)}, u32[]{:S(2)}, u32[]{:S(2)}) collective-permute-start(bf16[128,256]{1,0:T(8,128)(2,1)S(1)} %get-tuple-element.49), channel_id=1, source_target_pairs={{0,4},{4,8},{8,12},{12,16},{16,20},{20,24},{24,28},{28,32},{32,36}... | collective-permute-start | bytes 196616 | tf_op jit(solution)/shard_map/ppermute | solution.py:15
  73.9 5.4 %collective-permute-start.8 = (bf16[128,256]{1,0:T(8,128)(2,1)S(1)}, bf16[128,256]{1,0:T(8,128)(2,1)}, u32[]{:S(2)}, u32[]{:S(2)}) collective-permute-start(bf16[128,256]{1,0:T(8,128)(2,1)S(1)} %get-tuple-element.50), channel_id=1, source_target_pairs={{4,0},{8,4},{12,8},{16,12},{20,16},{24,20},{28,24},{32,28},{36,32}... | collective-permute-start | bytes 196616 | tf_op jit(solution)/shard_map/ppermute | solution.py:15
  79.4 1.6 %fusion.30 = f32[512,256]{0,1:T(8,128)S(1)} fusion(bf16[4096,256]{1,0:T(8,128)(2,1)S(1)} %copy-done.3, bf16[512,4096]{1,0:T(8,128)(2,1)S(1)} %copy-done.1, f32[4096]{0:T(1024)S(1)} %copy-done.4, f32[512]{0:T(512)S(1)} %add_rsqrt_fusion), kind=kOutput, calls=%fused_computation.59 | convolution fusion | flops 1082130432 | bytes 6834176 | tf_op jit(solution)/shard_map/dot_general | solution.py:42
  81.0 0.8 fusion.33
  82.0 1.2 copy.45
  83.2 1.6 %subtract_convert_fusion.1 = (bf16[512,2,64]{2,1,0:T(2,128)(2,1)S(1)}, bf16[512,2,64]{2,1,0:T(2,128)(2,1)S(1)}) fusion(f32[512,2,64]{2,1,0:T(2,128)S(1)} %copy.46, f32[512,2,64]{2,1,0:T(2,128)S(1)} %copy.45, f32[512,64]{1,0:T(8,128)} %copy.32, f32[512,64]{1,0:T(8,128)} %copy.30), kind=kLoop, calls=%fused_computation.24 | loop fusion | flops 524288 | bytes 1048576 | tf_op jit(solution)/shard_map/convert.2
  84.7 0.7 pad_maximum_fusion.3
  85.5 1.9 %collective-permute-start.2 = (bf16[512,256]{1,0:T(8,128)(2,1)S(1)}, bf16[512,256]{1,0:T(8,128)(2,1)S(1)}, u32[]{:S(2)}, u32[]{:S(2)}) collective-permute-start(bf16[512,256]{1,0:T(8,128)(2,1)S(1)} %bitcast.51), channel_id=1, source_target_pairs={{0,4},{4,8},{8,12},{12,16},{16,20},{20,24},{24,28},{28,32},{32,36}... | collective-permute-start | bytes 786440 | tf_op jit(solution)/shard_map/ppermute | solution.py:15
  87.4 5.9 %fusion.28 = f32[512,512]{0,1:T(8,128)S(1)} fusion(bf16[4096,512]{1,0:T(8,128)(2,1)} %param.9, bf16[512,4096]{1,0:T(8,128)(2,1)} %all-gather.2.cloned.1.call-done, f32[4096]{0:T(1024)} %param.8, f32[512]{0:T(512)S(1)} %add_rsqrt_fusion), kind=kOutput, calls=%fused_computation.58 | convolution fusion | flops 2155872256 | bytes 9455616 | tf_op jit(solution)/shard_map/dot_general | solution.py:41
  94.0 7.0 %collective-permute-start.6 = (bf16[128,256]{1,0:T(8,128)(2,1)S(1)}, bf16[128,256]{1,0:T(8,128)(2,1)S(1)}, u32[]{:S(2)}, u32[]{:S(2)}) collective-permute-start(bf16[128,256]{1,0:T(8,128)(2,1)S(1)} %bitcast.60), channel_id=1, source_target_pairs={{4,0},{8,4},{12,8},{16,12},{20,16},{24,20},{28,24},{32,28},{36,32}... | collective-permute-start | bytes 196616 | tf_op jit(solution)/shard_map/ppermute | solution.py:15
  100.9 2.1 %collective-permute-start.5 = (bf16[128,256]{1,0:T(8,128)(2,1)S(1)}, bf16[128,256]{1,0:T(8,128)(2,1)S(1)}, u32[]{:S(2)}, u32[]{:S(2)}) collective-permute-start(bf16[128,256]{1,0:T(8,128)(2,1)S(1)} %bitcast.59), channel_id=1, source_target_pairs={{0,4},{4,8},{8,12},{12,16},{16,20},{20,24},{24,28},{28,32},{32,36}... | collective-permute-start | bytes 196616 | tf_op jit(solution)/shard_map/ppermute | solution.py:15
  103.1 6.7 %collective-permute-done.5 = bf16[128,256]{1,0:T(8,128)(2,1)S(1)} collective-permute-done((bf16[128,256]{1,0:T(8,128)(2,1)S(1)}, bf16[128,256]{1,0:T(8,128)(2,1)S(1)}, u32[]{:S(2)}, u32[]{:S(2)}) %collective-permute-start.5) | collective-permute-done | bytes 65568 | tf_op jit(solution)/shard_map/ppermute | solution.py:15
  109.9 2.3 %maximum_select_fusion.1 = (bf16[768,256]{1,0:T(8,128)(2,1)}, bf16[768,256]{1,0:T(8,128)(2,1)S(1)}, bf16[768,256]{1,0:T(8,128)(2,1)S(1)}, bf16[768,256]{1,0:T(8,128)(2,1)}) fusion(bf16[128,256]{1,0:T(8,128)(2,1)} %collective-permute-done.8, bf16[512,256]{1,0:T(8,128)(2,1)} %convolution_convert_fusion, bf16[128,256]{1,0:T(8,128)(2,1)} %collective-permute-done.7, ...), kind=kLoop, calls=%fused_computation.28 | loop fusion | flops 4325376 | bytes 2884352 | tf_op jit(solution)/shard_map/jit(_where)/select_n | solution.py:137
  112.1 0.9 copy.42
  113.2 6.1 %fusion.36 = (f32[2,2,512]{2,1,0:T(2,128)S(1)}, f32[2,2,512,768]{2,3,1,0:T(8,128)}) fusion(pred[512,768]{0,1:T(8,128)(4,1)} %fusion.9, bf16[512,2,2,128]{0,3,2,1:T(8,128)(2,1)S(1)} %bitcast.53, bf16[768,2,128,1]{2,1,0,3:T(2,128)(2,1)S(1)} %bitcast.56), kind=kOutput, calls=%fused_computation.63 | convolution fusion | flops 408945408 | bytes 7610368 | tf_op jit(solution)/shard_map/while/body/eval_jaxpr/sub | solution.py:79
  119.3 3.4 %fusion.11 = bf16[512,2,2,128]{0,3,2,1:T(8,128)(2,1)S(1)} fusion(bf16[768,2,128,1]{0,2,3,1:T(8,128)(2,1)S(1)} %bitcast.55, f32[2,2,512,768]{2,3,1,0:T(8,128)} %get-tuple-element.60, f32[2,2,512]{2,1,0:T(2,128)S(1)} %get-tuple-element.59), kind=kOutput, calls=%fused_computation.17 | convolution fusion | flops 406061056 | bytes 7217152 | tf_op jit(solution)/shard_map/while/body/eval_jaxpr/gjrk,kgd->rgjd/dot_general | solution.py:81
  122.9 11.2 %all_to_all.19 = bf16[4,128,512]{1,2,0:T(8,128)(2,1)S(1)} all-to-all(bf16[4,128,512]{1,2,0:T(8,128)(2,1)S(1)} %copy.37), channel_id=1, replica_groups=mesh['seq'=64,'tp'=4] {'tp'}, dimensions={0} | all-to-all | bytes 1048576 | tf_op jit(solution)/shard_map/all_to_all | solution.py:138
  134.1 1.0 copy.38
  (47 shorter events, 5.0 us)
Async XLA Ops:
  7.2 58.2 %copy-start = (bf16[4096,256]{1,0:T(8,128)(2,1)S(1)}, bf16[4096,256]{1,0:T(8,128)(2,1)}, u32[]{:S(2)}) copy-start(bf16[4096,256]{1,0:T(8,128)(2,1)} %param.11) | copy-start | bytes 6291460
  7.2 58.2 %copy-start.4 = (f32[4096]{0:T(1024)S(1)}, f32[4096]{0:T(1024)}, u32[]{:S(2)}) copy-start(f32[4096]{0:T(1024)} %param.8) | copy-start | bytes 49156
  7.2 54.9 %all-gather.2.cloned.1.call-start = ((), (), s32[]{:S(2)}) async-start(), calls=%async_computation.1 | async-start | bytes 5242880 | tf_op jit(solution)/shard_map/all_gather | solution.py:91
  8.9 11.4 %collective-permute-start.4 = (s32[128]{0:T(128)S(1)}, s32[128]{0:T(128)S(1)}, u32[]{:S(2)}, u32[]{:S(2)}) collective-permute-start(s32[128]{0:T(128)S(1)} %slice.56), channel_id=1, source_target_pairs={{4,0},{8,4},{12,8},{16,12},{20,16},{24,20},{28,24},{32,28},{36,32}... | collective-permute-start | bytes 1544 | tf_op jit(solution)/shard_map/ppermute | solution.py:15
  12.7 8.2 %collective-permute-start.3 = (s32[128]{0:T(128)S(1)}, s32[128]{0:T(128)S(1)}, u32[]{:S(2)}, u32[]{:S(2)}) collective-permute-start(s32[128]{0:T(128)S(1)} %slice.54), channel_id=1, source_target_pairs={{0,4},{4,8},{8,12},{12,16},{16,20},{20,24},{24,28},{28,32},{32,36}... | collective-permute-start | bytes 1544 | tf_op jit(solution)/shard_map/ppermute | solution.py:15
  14.6 8.4 %collective-permute-start.1 = (s32[512]{0:T(512)}, s32[512]{0:T(512)S(1)}, u32[]{:S(2)}, u32[]{:S(2)}) collective-permute-start(s32[512]{0:T(512)} %param.12), channel_id=1, source_target_pairs={{0,4},{4,8},{8,12},{12,16},{16,20},{20,24},{24,28},{28,32},{32,36}... | collective-permute-start | bytes 6152 | tf_op jit(solution)/shard_map/ppermute | solution.py:15
  62.1 3.4 %copy-start.1 = (bf16[512,4096]{1,0:T(8,128)(2,1)S(1)}, bf16[512,4096]{1,0:T(8,128)(2,1)}, u32[]{:S(2)}) copy-start(bf16[512,4096]{1,0:T(8,128)(2,1)} %all-gather.2.cloned.1.call-done) | copy-start | bytes 12582916
  65.6 13.8 %copy-start.3 = (bf16[4096,256]{1,0:T(8,128)(2,1)S(1)}, bf16[4096,256]{1,0:T(8,128)(2,1)}, u32[]{:S(2)}) copy-start(bf16[4096,256]{1,0:T(8,128)(2,1)} %param.10) | copy-start | bytes 6291460
  68.5 41.3 %collective-permute-start = (bf16[512,256]{1,0:T(8,128)(2,1)}, bf16[512,256]{1,0:T(8,128)(2,1)}, u32[]{:S(2)}, u32[]{:S(2)}) collective-permute-start(bf16[512,256]{1,0:T(8,128)(2,1)} %convolution_convert_fusion), channel_id=1, source_target_pairs={{0,4},{4,8},{8,12},{12,16},{16,20},{20,24},{24,28},{28,32},{32,36}... | collective-permute-start | bytes 786440 | tf_op jit(solution)/shard_map/ppermute | solution.py:15
  70.5 30.5 %collective-permute-start.7 = (bf16[128,256]{1,0:T(8,128)(2,1)S(1)}, bf16[128,256]{1,0:T(8,128)(2,1)}, u32[]{:S(2)}, u32[]{:S(2)}) collective-permute-start(bf16[128,256]{1,0:T(8,128)(2,1)S(1)} %get-tuple-element.49), channel_id=1, source_target_pairs={{0,4},{4,8},{8,12},{12,16},{16,20},{20,24},{24,28},{28,32},{32,36}... | collective-permute-start | bytes 196616 | tf_op jit(solution)/shard_map/ppermute | solution.py:15
  73.9 29.2 %collective-permute-start.8 = (bf16[128,256]{1,0:T(8,128)(2,1)S(1)}, bf16[128,256]{1,0:T(8,128)(2,1)}, u32[]{:S(2)}, u32[]{:S(2)}) collective-permute-start(bf16[128,256]{1,0:T(8,128)(2,1)S(1)} %get-tuple-element.50), channel_id=1, source_target_pairs={{4,0},{8,4},{12,8},{16,12},{20,16},{24,20},{28,24},{32,28},{36,32}... | collective-permute-start | bytes 196616 | tf_op jit(solution)/shard_map/ppermute | solution.py:15
  85.5 24.4 %collective-permute-start.2 = (bf16[512,256]{1,0:T(8,128)(2,1)S(1)}, bf16[512,256]{1,0:T(8,128)(2,1)S(1)}, u32[]{:S(2)}, u32[]{:S(2)}) collective-permute-start(bf16[512,256]{1,0:T(8,128)(2,1)S(1)} %bitcast.51), channel_id=1, source_target_pairs={{0,4},{4,8},{8,12},{12,16},{16,20},{20,24},{24,28},{28,32},{32,36}... | collective-permute-start | bytes 786440 | tf_op jit(solution)/shard_map/ppermute | solution.py:15
  94.0 9.1 %collective-permute-start.6 = (bf16[128,256]{1,0:T(8,128)(2,1)S(1)}, bf16[128,256]{1,0:T(8,128)(2,1)S(1)}, u32[]{:S(2)}, u32[]{:S(2)}) collective-permute-start(bf16[128,256]{1,0:T(8,128)(2,1)S(1)} %bitcast.60), channel_id=1, source_target_pairs={{4,0},{8,4},{12,8},{16,12},{20,16},{24,20},{28,24},{32,28},{36,32}... | collective-permute-start | bytes 196616 | tf_op jit(solution)/shard_map/ppermute | solution.py:15
  100.9 8.9 %collective-permute-start.5 = (bf16[128,256]{1,0:T(8,128)(2,1)S(1)}, bf16[128,256]{1,0:T(8,128)(2,1)S(1)}, u32[]{:S(2)}, u32[]{:S(2)}) collective-permute-start(bf16[128,256]{1,0:T(8,128)(2,1)S(1)} %bitcast.59), channel_id=1, source_target_pairs={{0,4},{4,8},{8,12},{12,16},{16,20},{20,24},{24,28},{28,32},{32,36}... | collective-permute-start | bytes 196616 | tf_op jit(solution)/shard_map/ppermute | solution.py:15
  113.2 6.1 %copy-start.2 = (bf16[768,256]{0,1:T(8,128)(2,1)S(1)}, bf16[768,256]{0,1:T(8,128)(2,1)}, u32[]{:S(2)}) copy-start(bf16[768,256]{0,1:T(8,128)(2,1)} %copy.42) | copy-start | bytes 1179652
Sparse Core Ops, SparseCore 0:
  9.8 52.2 all-gather.1
where the time goes:
time: 143 us; the launch traced here: 142 us
  waiting for transfers between devices  46.3 us (32%)
  starting transfers between devices  29.3 us (20%)
  matrix products  19.1 us (13%)
  between operations  14.4 us (10%)
  other arithmetic  12.5 us (9%)
  blocking collectives  11.2 us (8%)
  local copies, waits for them, and re-layouts  9.14 us (6%)
    all_gather x1, waiting for transfers between devices, shards(): home_hidden = lax.all_gather(hidden, 'tp', axis=0, tiled=True)  36.2 us
    ppermute x9, starting transfers between devices, from_behind(): return lax.ppermute(array, axis, pairs)  29.3 us
    all_to_all x1, blocking collectives, shards(): lax.all_to_all(home_context, 'tp', split_axis=0, concat_axis=1, tiled=True)  11.2 us
    ppermute x9, waiting for transfers between devices, from_behind(): return lax.ppermute(array, axis, pairs)  9.44 us
    sub x1, matrix products, one_tile(): weights = jnp.exp(scores - highest)  6.09 us
    dot_general x1, matrix products, project(): queries = jnp.dot(normed, w_query, preferred_element_type=jnp.float32)  5.94 us
    dot_general x1, matrix products, one_tile(): jnp.einsum('gjrk,kgd->rgjd', weights, value_three, preferred_element_type...  3.37 us
    reduce_sum x1, other arithmetic, project(): jnp.mean(widened * widened, axis=1, keepdims=True) + EPS  3.23 us
  transfers between devices with their start and end apart: 10, of which 4 were waited for; matrix products, arithmetic and copies ran while one was open for 14% of the time, Pallas kernels for 0%

commit v1 on v0

--- a/solution.py
+++ b/solution.py
@@ -135,7 +135,19 @@
     live_column = frame_live[:, None] > 0
     key_cache = jnp.where(live_column, frame_keys, jnp.zeros((), jnp.bfloat16))
     value_cache = jnp.where(live_column, frame_values, jnp.zeros((), jnp.bfloat16))
-    context_rows = lax.all_to_all(home_context, "tp", split_axis=0, concat_axis=1, tiled=True)
+    ways, here = (lax.axis_size("tp"), lax.axis_index("tp"))
+    width = home_context.shape[0] // ways
+    dims = list(home_context.shape)
+    dims[0] = width
+    height = dims[1]
+    dims[1] = height * ways
+    full = jnp.zeros(dims, home_context.dtype)
+    for mask in range(ways):
+        part = lax.dynamic_slice_in_dim(home_context, (here ^ mask) * width, width, axis=0)
+        if mask:
+            part = lax.ppermute(part, "tp", [(d, d ^ mask) for d in range(ways)])
+        full = lax.dynamic_update_slice_in_dim(full, part, (here ^ mask) * height, axis=1)
+    context_rows = full
     return (context_rows, key_cache, value_cache)
 
 

time: 143 us -> 134 us (0.937)
  blocking collectives: 11.2 us -> 0 us
  starting transfers between devices: 29.3 us -> 37.6 us
  waiting for transfers between devices: 46.3 us -> 41.8 us
    all_to_all x1 -> x0, blocking collectives: 11.2 us -> none  [shards(): lax.all_to_all(home_context, 'tp', split_axis=0, concat_axis=1, tiled=True)]
    ppermute x9, waiting for transfers between devices: 9.44 us -> 4.32 us  [from_behind(): return lax.ppermute(array, axis, pairs)]
    ppermute x0 -> x3, starting transfers between devices: none -> 4.96 us  [shards(): part = lax.ppermute(part, 'tp', [(d, d ^ mask) for d in range(ways)])]
    ppermute x0 -> x3, waiting for transfers between devices: none -> 3.9 us  [shards(): part = lax.ppermute(part, 'tp', [(d, d ^ mask) for d in range(ways)])]
    dot_general x1, matrix products: 5.94 us -> 2.6 us  [project(): queries = jnp.dot(normed, w_query, preferred_element_type=jnp.float32)]
    ppermute x9, starting transfers between devices: 29.3 us -> 32.6 us  [from_behind(): return lax.ppermute(array, axis, pairs)]
    all_gather x1, waiting for transfers between devices: 36.2 us -> 32.9 us  [shards(): home_hidden = lax.all_gather(hidden, 'tp', axis=0, tiled=True)]
    dot_general x1, matrix products: 2.05 us -> 4.31 us  [project(): values_f = jnp.dot(normed, w_value, preferred_element_type=jnp.float32)]
  transfers between devices with their start and end apart: 10 -> 13, of which waited for: 4 -> 5; matrix products, arithmetic and copies ran while one was open for 14% -> 8% of each run, Pallas kernels for 0% -> 0%
where the time goes in v1:
time: 134 us; the launch traced here: 132 us
  waiting for transfers between devices  41.8 us (31%)
  starting transfers between devices  37.6 us (28%)
  matrix products  18 us (13%)
  between operations  14.5 us (11%)
  other arithmetic  11.3 us (8%)
  local copies, waits for them, and re-layouts  8.54 us (6%)
    all_gather x1, waiting for transfers between devices, shards(): home_hidden = lax.all_gather(hidden, 'tp', axis=0, tiled=True)  32.9 us
    ppermute x9, starting transfers between devices, from_behind(): return lax.ppermute(array, axis, pairs)  32.6 us
    sub x1, matrix products, one_tile(): weights = jnp.exp(scores - highest)  6.16 us
    ppermute x3, starting transfers between devices, shards(): part = lax.ppermute(part, 'tp', [(d, d ^ mask) for d in range(ways)])  4.96 us
    ppermute x9, waiting for transfers between devices, from_behind(): return lax.ppermute(array, axis, pairs)  4.32 us
    dot_general x1, matrix products, project(): values_f = jnp.dot(normed, w_value, preferred_element_type=jnp.float32)  4.31 us
    ppermute x3, waiting for transfers between devices, shards(): part = lax.ppermute(part, 'tp', [(d, d ^ mask) for d in range(ways)])  3.9 us
    dot_general x1, matrix products, one_tile(): jnp.einsum('gjrk,kgd->rgjd', weights, value_three, preferred_element_type...  3.37 us
  transfers between devices with their start and end apart: 13, of which 5 were waited for; matrix products, arithmetic and copies ran while one was open for 8% of the time, Pallas kernels for 0%

profile of v1, /device:TPU:128, one launch (start us, length us, event | category | flops | bytes accessed | tf_op | source)
XLA Modules:
  0.0 131.8 jit_solution(3380435688488272077)
XLA Ops:
  7.9 0.8 fusion.34
  8.9 1.9 %collective-permute-start.6 = (s32[128]{0:T(128)S(1)}, s32[128]{0:T(128)S(1)}, u32[]{:S(2)}, u32[]{:S(2)}) collective-permute-start(s32[128]{0:T(128)S(1)} %slice.54), channel_id=1, source_target_pairs={{0,4},{4,8},{8,12},{12,16},{16,20},{20,24},{24,28},{28,32},{32,36}... | collective-permute-start | bytes 1544 | tf_op jit(solution)/shard_map/ppermute | solution.py:15
  11.0 7.0 %collective-permute-start.7 = (s32[128]{0:T(128)S(1)}, s32[128]{0:T(128)S(1)}, u32[]{:S(2)}, u32[]{:S(2)}) collective-permute-start(s32[128]{0:T(128)S(1)} %slice.56), channel_id=1, source_target_pairs={{4,0},{8,4},{12,8},{16,12},{20,16},{24,20},{28,24},{32,28},{36,32}... | collective-permute-start | bytes 1544 | tf_op jit(solution)/shard_map/ppermute | solution.py:15
  17.9 1.9 %collective-permute-start.1 = (s32[512]{0:T(512)}, s32[512]{0:T(512)S(1)}, u32[]{:S(2)}, u32[]{:S(2)}) collective-permute-start(s32[512]{0:T(512)} %param.12), channel_id=1, source_target_pairs={{0,4},{4,8},{8,12},{12,16},{16,20},{20,24},{24,28},{28,32},{32,36}... | collective-permute-start | bytes 6152 | tf_op jit(solution)/shard_map/ppermute | solution.py:15
  21.1 0.8 copy.23
  22.0 0.8 copy.25
  23.7 2.7 %collective-permute-done.1 = s32[512]{0:T(512)S(1)} collective-permute-done((s32[512]{0:T(512)}, s32[512]{0:T(512)S(1)}, u32[]{:S(2)}, u32[]{:S(2)}) %collective-permute-start.1) | collective-permute-done | bytes 2080 | tf_op jit(solution)/shard_map/ppermute | solution.py:15
  27.1 2.2 %fusion.9 = pred[512,768]{0,1:T(8,128)(4,1)} fusion(s32[512]{0:T(512)S(1)} %iota_add_fusion.1, s32[512]{0:T(512)S(1)} %get-tuple-element.60, s32[512]{0:T(512)} %param.12, s32[768]{0:T(1024)S(1)} %dynamic_slice.37, s32[768]{0:T(1024)S(1)} %dynamic_slice.36, pred[768]{0:T(1024)(128)(4,1)S(1)} %slice_compare_fusion), kind=kLoop, calls=%fused_computation.15 | loop fusion | flops 2359296 | bytes 406272 | tf_op jit(solution)/shard_map/while/body/eval_jaxpr/or | solution.py:76
  29.2 32.9 %all-gather.2.cloned.1.call-done = bf16[512,4096]{1,0:T(8,128)(2,1)} async-done(((bf16[128,4096]{1,0:T(8,128)(2,1)}), bf16[512,4096]{1,0:T(8,128)(2,1)}) %all-gather.2.cloned.1.call-update) | async-done | bytes 4194320 | tf_op jit(solution)/shard_map/all_gather | solution.py:91
  62.1 3.2 %fusion.1 = f32[512]{0:T(512)S(1)} fusion(bf16[512,4096]{1,0:T(8,128)(2,1)} %all-gather.2.cloned.1.call-done), kind=kLoop, calls=%fused_computation.3 | loop fusion | flops 6290944 | bytes 4196352 | tf_op jit(solution)/shard_map/reduce_sum | solution.py:39
  65.6 1.6 %fusion.29 = f32[512,256]{0,1:T(8,128)S(1)} fusion(bf16[4096,256]{1,0:T(8,128)(2,1)S(1)} %copy-done, bf16[512,4096]{1,0:T(8,128)(2,1)S(1)} %copy-done.1, f32[4096]{0:T(1024)S(1)} %copy-done.5, f32[512]{0:T(512)S(1)} %add_rsqrt_fusion), kind=kOutput, calls=%fused_computation.66 | convolution fusion | flops 1082130432 | bytes 6834176 | tf_op jit(solution)/shard_map/dot_general | solution.py:42
  68.2 1.2 copy.41
  69.4 1.6 %subtract_convert_fusion.1 = (bf16[512,2,64]{2,1,0:T(2,128)(2,1)S(1)}, bf16[512,2,64]{2,1,0:T(2,128)(2,1)S(1)}) fusion(f32[512,2,64]{2,1,0:T(2,128)S(1)} %copy.41, f32[512,2,64]{2,1,0:T(2,128)S(1)} %copy.40, f32[512,64]{1,0:T(8,128)} %copy.25, f32[512,64]{1,0:T(8,128)} %copy.23), kind=kLoop, calls=%fused_computation.23 | loop fusion | flops 524288 | bytes 1048576 | tf_op jit(solution)/shard_map/convert.2
  72.1 4.3 %convolution_convert_fusion = bf16[512,256]{1,0:T(8,128)(2,1)S(1)} fusion(bf16[4096,256]{1,0:T(8,128)(2,1)} %param.11, bf16[512,4096]{1,0:T(8,128)(2,1)} %all-gather.2.cloned.1.call-done, f32[4096]{0:T(1024)S(1)} %copy-done.5, f32[512]{0:T(512)S(1)} %add_rsqrt_fusion), kind=kOutput, calls=%fused_computation.17 | convolution fusion | flops 1082261504 | bytes 6572032 | tf_op jit(solution)/shard_map/dot_general | solution.py:43
  76.4 1.9 %collective-permute-start = (bf16[512,256]{1,0:T(8,128)(2,1)S(1)}, bf16[512,256]{1,0:T(8,128)(2,1)S(1)}, u32[]{:S(2)}, u32[]{:S(2)}) collective-permute-start(bf16[512,256]{1,0:T(8,128)(2,1)S(1)} %convolution_convert_fusion), channel_id=1, source_target_pairs={{0,4},{4,8},{8,12},{12,16},{16,20},{20,24},{24,28},{28,32},{32,36}... | collective-permute-start | bytes 786440 | tf_op jit(solution)/shard_map/ppermute | solution.py:15
  78.3 3.5 %collective-permute-start.8 = (bf16[128,256]{1,0:T(8,128)(2,1)S(1)}, bf16[128,256]{1,0:T(8,128)(2,1)S(1)}, u32[]{:S(2)}, u32[]{:S(2)}) collective-permute-start(bf16[128,256]{1,0:T(8,128)(2,1)S(1)} %bitcast.54), channel_id=1, source_target_pairs={{0,4},{4,8},{8,12},{12,16},{16,20},{20,24},{24,28},{28,32},{32,36}... | collective-permute-start | bytes 196616 | tf_op jit(solution)/shard_map/ppermute | solution.py:15
  81.8 5.4 %collective-permute-start.9 = (bf16[128,256]{1,0:T(8,128)(2,1)S(1)}, bf16[128,256]{1,0:T(8,128)(2,1)S(1)}, u32[]{:S(2)}, u32[]{:S(2)}) collective-permute-start(bf16[128,256]{1,0:T(8,128)(2,1)S(1)} %bitcast.53), channel_id=1, source_target_pairs={{4,0},{8,4},{12,8},{16,12},{20,16},{24,20},{28,24},{32,28},{36,32}... | collective-permute-start | bytes 196616 | tf_op jit(solution)/shard_map/ppermute | solution.py:15
  87.3 1.9 %collective-permute-start.2 = (bf16[512,256]{1,0:T(8,128)(2,1)S(1)}, bf16[512,256]{1,0:T(8,128)(2,1)S(1)}, u32[]{:S(2)}, u32[]{:S(2)}) collective-permute-start(bf16[512,256]{1,0:T(8,128)(2,1)S(1)} %bitcast.44), channel_id=1, source_target_pairs={{0,4},{4,8},{8,12},{12,16},{16,20},{20,24},{24,28},{28,32},{32,36}... | collective-permute-start | bytes 786440 | tf_op jit(solution)/shard_map/ppermute | solution.py:15
  89.2 1.9 %collective-permute-start.10 = (bf16[128,256]{1,0:T(8,128)(2,1)S(1)}, bf16[128,256]{1,0:T(8,128)(2,1)S(1)}, u32[]{:S(2)}, u32[]{:S(2)}) collective-permute-start(bf16[128,256]{1,0:T(8,128)(2,1)S(1)} %get-tuple-element.47), channel_id=1, source_target_pairs={{0,4},{4,8},{8,12},{12,16},{16,20},{20,24},{24,28},{28,32},{32,36}... | collective-permute-start | bytes 196616 | tf_op jit(solution)/shard_map/ppermute | solution.py:15
  91.2 2.6 %fusion.27 = f32[512,512]{0,1:T(8,128)S(1)} fusion(bf16[4096,512]{1,0:T(8,128)(2,1)S(1)} %copy-done.4, bf16[512,4096]{1,0:T(8,128)(2,1)S(1)} %copy-done.2, f32[4096]{0:T(1024)S(1)} %copy-done.5, f32[512]{0:T(512)S(1)} %add_rsqrt_fusion), kind=kOutput, calls=%fused_computation.65 | convolution fusion | flops 2155872256 | bytes 9455616 | tf_op jit(solution)/shard_map/dot_general | solution.py:41
  94.0 7.1 %collective-permute-start.11 = (bf16[128,256]{1,0:T(8,128)(2,1)S(1)}, bf16[128,256]{1,0:T(8,128)(2,1)S(1)}, u32[]{:S(2)}, u32[]{:S(2)}) collective-permute-start(bf16[128,256]{1,0:T(8,128)(2,1)S(1)} %get-tuple-element.48), channel_id=1, source_target_pairs={{4,0},{8,4},{12,8},{16,12},{20,16},{24,20},{28,24},{32,28},{36,32}... | collective-permute-start | bytes 196616 | tf_op jit(solution)/shard_map/ppermute | solution.py:15
  101.2 1.6 %collective-permute-done.11 = bf16[128,256]{1,0:T(8,128)(2,1)S(1)} collective-permute-done((bf16[128,256]{1,0:T(8,128)(2,1)S(1)}, bf16[128,256]{1,0:T(8,128)(2,1)S(1)}, u32[]{:S(2)}, u32[]{:S(2)}) %collective-permute-start.11) | collective-permute-done | bytes 65568 | tf_op jit(solution)/shard_map/ppermute | solution.py:15
  102.9 1.1 maximum_select_fusion.1
  104.0 0.8 reshape.239
  105.0 6.2 %fusion.35 = (f32[2,2,512]{2,1,0:T(2,128)S(1)}, f32[2,2,512,768]{2,3,1,0:T(8,128)}) fusion(pred[512,768]{0,1:T(8,128)(4,1)} %fusion.9, bf16[512,2,2,128]{0,3,2,1:T(8,128)(2,1)S(1)} %bitcast.46, bf16[768,2,128,1]{2,1,0,3:T(2,128)(2,1)} %bitcast.50), kind=kOutput, calls=%fused_computation.70 | convolution fusion | flops 408945408 | bytes 7610368 | tf_op jit(solution)/shard_map/while/body/eval_jaxpr/sub | solution.py:79
  111.2 3.4 %fusion.10 = bf16[2,128,2,512]{3,1,2,0:T(8,128)(2,1)S(1)} fusion(bf16[768,2,128,1]{0,2,3,1:T(8,128)(2,1)S(1)} %bitcast.49, f32[2,2,512,768]{2,3,1,0:T(8,128)} %get-tuple-element.58, f32[2,2,512]{2,1,0:T(2,128)S(1)} %get-tuple-element.57), kind=kOutput, calls=%fused_computation.16 | convolution fusion | flops 406061056 | bytes 7217152 | tf_op jit(solution)/shard_map/while/body/eval_jaxpr/gjrk,kgd->rgjd/dot_general | solution.py:81
  114.8 0.9 collective-permute-start.3
  115.9 1.8 %collective-permute-start.4 = (bf16[128,512]{1,0:T(8,128)(2,1)S(1)}, bf16[128,512]{1,0:T(8,128)(2,1)S(1)}, u32[]{:S(2)}, u32[]{:S(2)}) collective-permute-start(bf16[128,512]{1,0:T(8,128)(2,1)S(1)} %copy.44), channel_id=1, source_target_pairs={{0,2},{1,3},{2,0},{3,1},{4,6},{5,7},{6,4},{7,5},{8,10},{9,11},{10,... | collective-permute-start | bytes 393224 | tf_op jit(solution)/shard_map/ppermute | solution.py:148
  117.9 2.2 %collective-permute-start.5 = (bf16[128,512]{1,0:T(8,128)(2,1)S(1)}, bf16[128,512]{1,0:T(8,128)(2,1)S(1)}, u32[]{:S(2)}, u32[]{:S(2)}) collective-permute-start(bf16[128,512]{1,0:T(8,128)(2,1)S(1)} %copy.45), channel_id=1, source_target_pairs={{0,3},{1,2},{2,1},{3,0},{4,7},{5,6},{6,5},{7,4},{8,11},{9,10},{10,... | collective-permute-start | bytes 393224 | tf_op jit(solution)/shard_map/ppermute | solution.py:148
  120.2 2.3 %collective-permute-done.4 = bf16[128,512]{1,0:T(8,128)(2,1)S(1)} collective-permute-done((bf16[128,512]{1,0:T(8,128)(2,1)S(1)}, bf16[128,512]{1,0:T(8,128)(2,1)S(1)}, u32[]{:S(2)}, u32[]{:S(2)}) %collective-permute-start.4) | collective-permute-done | bytes 131104 | tf_op jit(solution)/shard_map/ppermute | solution.py:148
  122.5 1.6 %collective-permute-done.5 = bf16[128,512]{1,0:T(8,128)(2,1)S(1)} collective-permute-done((bf16[128,512]{1,0:T(8,128)(2,1)S(1)}, bf16[128,512]{1,0:T(8,128)(2,1)S(1)}, u32[]{:S(2)}, u32[]{:S(2)}) %collective-permute-start.5) | collective-permute-done | bytes 131104 | tf_op jit(solution)/shard_map/ppermute | solution.py:148
  124.2 0.8 copy-done.3
  (61 shorter events, 7.2 us)
Async XLA Ops:
  7.2 58.2 %copy-start = (bf16[4096,256]{1,0:T(8,128)(2,1)S(1)}, bf16[4096,256]{1,0:T(8,128)(2,1)}, u32[]{:S(2)}) copy-start(bf16[4096,256]{1,0:T(8,128)(2,1)} %param.10) | copy-start | bytes 6291460
  7.2 58.2 %copy-start.5 = (f32[4096]{0:T(1024)S(1)}, f32[4096]{0:T(1024)}, u32[]{:S(2)}) copy-start(f32[4096]{0:T(1024)} %param.8) | copy-start | bytes 49156
  7.2 54.9 %all-gather.2.cloned.1.call-start = ((), (), s32[]{:S(2)}) async-start(), calls=%async_computation | async-start | bytes 5242880 | tf_op jit(solution)/shard_map/all_gather | solution.py:91
  8.9 14.8 %collective-permute-start.6 = (s32[128]{0:T(128)S(1)}, s32[128]{0:T(128)S(1)}, u32[]{:S(2)}, u32[]{:S(2)}) collective-permute-start(s32[128]{0:T(128)S(1)} %slice.54), channel_id=1, source_target_pairs={{0,4},{4,8},{8,12},{12,16},{16,20},{20,24},{24,28},{28,32},{32,36}... | collective-permute-start | bytes 1544 | tf_op jit(solution)/shard_map/ppermute | solution.py:15
  11.0 12.7 %collective-permute-start.7 = (s32[128]{0:T(128)S(1)}, s32[128]{0:T(128)S(1)}, u32[]{:S(2)}, u32[]{:S(2)}) collective-permute-start(s32[128]{0:T(128)S(1)} %slice.56), channel_id=1, source_target_pairs={{4,0},{8,4},{12,8},{16,12},{20,16},{24,20},{28,24},{32,28},{36,32}... | collective-permute-start | bytes 1544 | tf_op jit(solution)/shard_map/ppermute | solution.py:15
  17.9 8.4 %collective-permute-start.1 = (s32[512]{0:T(512)}, s32[512]{0:T(512)S(1)}, u32[]{:S(2)}, u32[]{:S(2)}) collective-permute-start(s32[512]{0:T(512)} %param.12), channel_id=1, source_target_pairs={{0,4},{4,8},{8,12},{12,16},{16,20},{20,24},{24,28},{28,32},{32,36}... | collective-permute-start | bytes 6152 | tf_op jit(solution)/shard_map/ppermute | solution.py:15
  62.1 3.4 %copy-start.1 = (bf16[512,4096]{1,0:T(8,128)(2,1)S(1)}, bf16[512,4096]{1,0:T(8,128)(2,1)}, u32[]{:S(2)}) copy-start(bf16[512,4096]{1,0:T(8,128)(2,1)} %all-gather.2.cloned.1.call-done) | copy-start | bytes 12582916
  72.0 19.1 %copy-start.2 = (bf16[512,4096]{1,0:T(8,128)(2,1)S(1)}, bf16[512,4096]{1,0:T(8,128)(2,1)}, u32[]{:S(2)}) copy-start(bf16[512,4096]{1,0:T(8,128)(2,1)} %all-gather.2.cloned.1.call-done) | copy-start | bytes 12582916
  72.0 19.1 %copy-start.4 = (bf16[4096,512]{1,0:T(8,128)(2,1)S(1)}, bf16[4096,512]{1,0:T(8,128)(2,1)}, u32[]{:S(2)}) copy-start(bf16[4096,512]{1,0:T(8,128)(2,1)} %param.9) | copy-start | bytes 12582916
  76.4 26.5 %collective-permute-start = (bf16[512,256]{1,0:T(8,128)(2,1)S(1)}, bf16[512,256]{1,0:T(8,128)(2,1)S(1)}, u32[]{:S(2)}, u32[]{:S(2)}) collective-permute-start(bf16[512,256]{1,0:T(8,128)(2,1)S(1)} %convolution_convert_fusion), channel_id=1, source_target_pairs={{0,4},{4,8},{8,12},{12,16},{16,20},{20,24},{24,28},{28,32},{32,36}... | collective-permute-start | bytes 786440 | tf_op jit(solution)/shard_map/ppermute | solution.py:15
  78.3 15.6 %collective-permute-start.8 = (bf16[128,256]{1,0:T(8,128)(2,1)S(1)}, bf16[128,256]{1,0:T(8,128)(2,1)S(1)}, u32[]{:S(2)}, u32[]{:S(2)}) collective-permute-start(bf16[128,256]{1,0:T(8,128)(2,1)S(1)} %bitcast.54), channel_id=1, source_target_pairs={{0,4},{4,8},{8,12},{12,16},{16,20},{20,24},{24,28},{28,32},{32,36}... | collective-permute-start | bytes 196616 | tf_op jit(solution)/shard_map/ppermute | solution.py:15
  81.8 19.3 %collective-permute-start.9 = (bf16[128,256]{1,0:T(8,128)(2,1)S(1)}, bf16[128,256]{1,0:T(8,128)(2,1)S(1)}, u32[]{:S(2)}, u32[]{:S(2)}) collective-permute-start(bf16[128,256]{1,0:T(8,128)(2,1)S(1)} %bitcast.53), channel_id=1, source_target_pairs={{4,0},{8,4},{12,8},{16,12},{20,16},{24,20},{28,24},{32,28},{36,32}... | collective-permute-start | bytes 196616 | tf_op jit(solution)/shard_map/ppermute | solution.py:15
  87.3 15.5 %collective-permute-start.2 = (bf16[512,256]{1,0:T(8,128)(2,1)S(1)}, bf16[512,256]{1,0:T(8,128)(2,1)S(1)}, u32[]{:S(2)}, u32[]{:S(2)}) collective-permute-start(bf16[512,256]{1,0:T(8,128)(2,1)S(1)} %bitcast.44), channel_id=1, source_target_pairs={{0,4},{4,8},{8,12},{12,16},{16,20},{20,24},{24,28},{28,32},{32,36}... | collective-permute-start | bytes 786440 | tf_op jit(solution)/shard_map/ppermute | solution.py:15
  89.2 12.0 %collective-permute-start.10 = (bf16[128,256]{1,0:T(8,128)(2,1)S(1)}, bf16[128,256]{1,0:T(8,128)(2,1)S(1)}, u32[]{:S(2)}, u32[]{:S(2)}) collective-permute-start(bf16[128,256]{1,0:T(8,128)(2,1)S(1)} %get-tuple-element.47), channel_id=1, source_target_pairs={{0,4},{4,8},{8,12},{12,16},{16,20},{20,24},{24,28},{28,32},{32,36}... | collective-permute-start | bytes 196616 | tf_op jit(solution)/shard_map/ppermute | solution.py:15
  94.0 8.9 %collective-permute-start.11 = (bf16[128,256]{1,0:T(8,128)(2,1)S(1)}, bf16[128,256]{1,0:T(8,128)(2,1)S(1)}, u32[]{:S(2)}, u32[]{:S(2)}) collective-permute-start(bf16[128,256]{1,0:T(8,128)(2,1)S(1)} %get-tuple-element.48), channel_id=1, source_target_pairs={{4,0},{8,4},{12,8},{16,12},{20,16},{24,20},{28,24},{32,28},{36,32}... | collective-permute-start | bytes 196616 | tf_op jit(solution)/shard_map/ppermute | solution.py:15
  114.8 5.4 %collective-permute-start.3 = (bf16[128,512]{1,0:T(8,128)(2,1)S(1)}, bf16[128,512]{1,0:T(8,128)(2,1)S(1)}, u32[]{:S(2)}, u32[]{:S(2)}) collective-permute-start(bf16[128,512]{1,0:T(8,128)(2,1)S(1)} %copy.43), channel_id=1, source_target_pairs={{0,1},{1,0},{2,3},{3,2},{4,5},{5,4},{6,7},{7,6},{8,9},{9,8},{10,11... | collective-permute-start | bytes 393224 | tf_op jit(solution)/shard_map/ppermute | solution.py:148
  115.9 6.6 %collective-permute-start.4 = (bf16[128,512]{1,0:T(8,128)(2,1)S(1)}, bf16[128,512]{1,0:T(8,128)(2,1)S(1)}, u32[]{:S(2)}, u32[]{:S(2)}) collective-permute-start(bf16[128,512]{1,0:T(8,128)(2,1)S(1)} %copy.44), channel_id=1, source_target_pairs={{0,2},{1,3},{2,0},{3,1},{4,6},{5,7},{6,4},{7,5},{8,10},{9,11},{10,... | collective-permute-start | bytes 393224 | tf_op jit(solution)/shard_map/ppermute | solution.py:148
  117.9 6.3 %collective-permute-start.5 = (bf16[128,512]{1,0:T(8,128)(2,1)S(1)}, bf16[128,512]{1,0:T(8,128)(2,1)S(1)}, u32[]{:S(2)}, u32[]{:S(2)}) collective-permute-start(bf16[128,512]{1,0:T(8,128)(2,1)S(1)} %copy.45), channel_id=1, source_target_pairs={{0,3},{1,2},{2,1},{3,0},{4,7},{5,6},{6,5},{7,4},{8,11},{9,10},{10,... | collective-permute-start | bytes 393224 | tf_op jit(solution)/shard_map/ppermute | solution.py:148
  124.1 0.8 copy-start.3
Sparse Core Ops, SparseCore 0:
  9.8 52.2 all-gather.1
